TPU v7x, 512 devices: a whole 4x8x8 slice. The times are simulated.
512 devices in a mesh: ctx: 64 (over z_lo, y, core), head: 8 (over z_hi, x).
Axes of the slice: x: 4, y: 8, z: 8 (z_hi: 2, z_lo: 4; z = z_hi * 4 + z_lo), core: 2. Of those that a mesh axis runs over, the one named last changes fastest.
Arguments:
- frozen_queries: bfloat16 [8192, 12288], P('ctx', 'head'), may hold values from -20.4 to 20.4
- query_latent_rows: bfloat16 [8192, 1536], P('ctx'), may hold values from -6 to 6
- key_value_latent: bfloat16 [8192, 576], P('ctx'), may hold values from -20.4 to 20.4
- block_starts: int32 [64, 2], P('ctx'), may hold values from 0 to 960, as said below
- latent_up_weight: bfloat16 [512, 16384], P(None, 'head'), may hold values from -0.25 to 0.25
- query_adapter_first: bfloat16 [1536, 32], replicated, may hold values from -0.15625 to 0.15625
- query_adapter_second: bfloat16 [32, 12288], P(None, 'head'), may hold values from -1 to 1
- output_adapter_first: bfloat16 [8192, 32], P('head'), may hold values from -0.0625 to 0.0625
- output_adapter_second: bfloat16 [32, 2560], replicated, may hold values from -1 to 1
- frozen_output_weight: bfloat16 [8192, 2560], P('head', 'ctx'), may hold values from -0.0625 to 0.0625
- output_cotangent: bfloat16 [8192, 2560], P('ctx'), may hold values from -0.1875 to 0.1875
Outputs:
- grad_qa: float32 [1536, 32], replicated
- grad_qb: float32 [32, 12288], P(None, 'head')
- grad_oa: float32 [8192, 32], P('head')
- grad_ob: float32 [32, 2560], P(None, 'ctx')
Inputs may be any that keep to these rules, and one draw needn't show every extreme that they name: For c < 8, each of the 8 groups of one sequence holds block_starts = (c * 64, (15 - c) * 64), every c once per sequence.
All inputs are finite; a program needn't handle non-finite values.
Results may differ from a plain program's by a relative error of at most 0.02.
The roundings to bfloat16 on the way count: a program that leaves them out, or rounds other values in their place, can miss the bound.
Values may be sent and summed in bfloat16 or wider, within the bound.
A program may use at most 128 MiB of HBM per device.

v0:
```python
import jax
import jax.numpy as jnp
from jax import lax
from jax.sharding import PartitionSpec as P

PLAIN_WIDTH = 128
ROTARY_WIDTH = 64
VALUE_WIDTH = 128
KVL = 512
SPAN = 8
ROPE_BASE = 10000.0


def passed_along(value, axis, steps):
    count = lax.axis_size(axis)
    pairs = [(source, (source + steps) % count) for source in range(count)]
    return lax.ppermute(value, axis, pairs)


def rotate(vectors, positions, sign):
    half_width = vectors.shape[-1] // 2
    freq = ROPE_BASE ** (-jnp.arange(half_width, dtype=jnp.float32) * 2.0 / vectors.shape[-1])
    angle = positions.astype(jnp.float32)[..., None] * freq
    angle = angle.reshape(
        positions.shape + (1,) * (vectors.ndim - positions.ndim - 1) + (half_width,)
    )
    cosine = jnp.cos(angle)
    sine = jnp.sin(angle) * sign
    first = vectors[..., :half_width]
    second = vectors[..., half_width:]
    return jnp.concatenate([first * cosine - second * sine, second * cosine + first * sine], -1)


def block_positions(offsets, half_rows):
    steps = jnp.arange(half_rows, dtype=jnp.int32)
    return jnp.concatenate([offsets[0] + steps, offsets[1] + steps])


def expand_block(latent_rows, latent_up_weight, positions):
    kv_up = jnp.dot(
        latent_rows[:, :KVL], latent_up_weight, preferred_element_type=jnp.float32
    ).astype(jnp.bfloat16)
    rope_key = rotate(latent_rows[:, KVL:].astype(jnp.float32), positions, 1.0).astype(jnp.bfloat16)
    return jnp.concatenate([kv_up, rope_key], -1)


def block_scores(query_full, block, head_number):
    split = head_number * (PLAIN_WIDTH + VALUE_WIDTH)
    kv_heads = block[:, :split].reshape(block.shape[0], head_number, PLAIN_WIDTH + VALUE_WIDTH)
    nope_part = jnp.einsum(
        "qhd,khd->hqk",
        query_full[..., :PLAIN_WIDTH],
        kv_heads[..., :PLAIN_WIDTH],
        preferred_element_type=jnp.float32,
    )
    rope_part = jnp.einsum(
        "qhd,kd->hqk",
        query_full[..., PLAIN_WIDTH:],
        block[:, split:],
        preferred_element_type=jnp.float32,
    )
    return nope_part + rope_part


def contract_rows(left, right):
    return lax.dot_general(
        left, right, (((0,), (0,)), ((), ())), preferred_element_type=jnp.float32
    )


def columns_contract(left, right):
    return lax.dot_general(
        left, right, (((1,), (1,)), ((), ())), preferred_element_type=jnp.float32
    )


def body(
    frozen_queries,
    query_latent_rows,
    key_value_latent,
    block_starts,
    latent_up_weight,
    query_adapter_first,
    query_adapter_second,
    output_adapter_first,
    output_adapter_second,
    frozen_output_weight,
    output_cotangent,
):
    token_rows = frozen_queries.shape[0]
    half_rows = token_rows // 2
    per_head_width = PLAIN_WIDTH + ROTARY_WIDTH
    head_number = query_adapter_second.shape[1] // per_head_width
    score_scale = per_head_width ** (-0.5)
    axis_count = lax.axis_size("ctx")
    stride = axis_count // SPAN
    axis_place = lax.axis_index("ctx")
    all_offsets = lax.all_gather(block_starts, "ctx", axis=0, tiled=True)
    own_positions = block_positions(block_starts[0], half_rows)
    query_rank_rows = jnp.dot(
        query_latent_rows, query_adapter_first, preferred_element_type=jnp.float32
    ).astype(jnp.bfloat16)
    query_full = frozen_queries.astype(jnp.float32) + jnp.dot(
        query_rank_rows, query_adapter_second, preferred_element_type=jnp.float32
    )
    query_full = query_full.reshape(token_rows, head_number, per_head_width)
    query_full = jnp.concatenate(
        [query_full[..., :PLAIN_WIDTH], rotate(query_full[..., PLAIN_WIDTH:], own_positions, 1.0)],
        -1,
    ).astype(jnp.bfloat16)

    def prepare(block, positions):
        return expand_block(block, latent_up_weight, positions)

    collected = []

    def take(block, distance):
        source = (axis_place - distance * stride) % axis_count
        source_offsets = lax.dynamic_index_in_dim(all_offsets, source, 0, keepdims=False)
        positions = block_positions(source_offsets, half_rows)
        expanded = prepare(block, positions)
        collected.append((expanded, positions, block_scores(query_full, expanded, head_number)))

    take(key_value_latent, 0)
    moving = key_value_latent
    for hop in range(1, SPAN):
        moving = passed_along(moving, "ctx", stride)
        take(moving, hop)
    kv_all = jnp.concatenate([entry[0] for entry in collected], 0)
    key_positions = jnp.concatenate([entry[1] for entry in collected], 0)
    scores = jnp.concatenate([entry[2] for entry in collected], -1) * score_scale
    causal = key_positions[None, :] <= own_positions[:, None]
    scores = jnp.where(causal[None], scores, -jnp.inf)
    top = jnp.max(scores, -1, keepdims=True)
    expo = jnp.exp(scores - top)
    weights = (expo / jnp.sum(expo, -1, keepdims=True)).astype(jnp.bfloat16)
    split = head_number * (PLAIN_WIDTH + VALUE_WIDTH)
    key_count = kv_all.shape[0]
    kv_heads = kv_all[:, :split].reshape(key_count, head_number, PLAIN_WIDTH + VALUE_WIDTH)
    key_nope = kv_heads[..., :PLAIN_WIDTH]
    values = kv_heads[..., PLAIN_WIDTH:]
    rope_keys = kv_all[:, split:]
    attended_values = jnp.einsum(
        "hqk,khv->qhv", weights, values, preferred_element_type=jnp.float32
    ).astype(jnp.bfloat16)
    attended_flattened = attended_values.reshape(token_rows, head_number * VALUE_WIDTH)
    output_partial_sum = jnp.dot(
        attended_flattened, output_adapter_first, preferred_element_type=jnp.float32
    )
    output_rank_rows = lax.psum(output_partial_sum, "head").astype(jnp.bfloat16)
    output_rank_gradient = columns_contract(output_cotangent, output_adapter_second).astype(
        jnp.bfloat16
    )
    grad_ob = lax.psum_scatter(
        contract_rows(output_rank_rows, output_cotangent), "ctx", scatter_dimension=1, tiled=True
    )
    grad_oa = lax.psum(contract_rows(attended_flattened, output_rank_gradient), "ctx")
    frozen_query_gradient = columns_contract(
        output_cotangent, lax.all_gather(frozen_output_weight, "ctx", axis=1, tiled=True)
    )
    attended_gradient = (
        (frozen_query_gradient + columns_contract(output_rank_gradient, output_adapter_first))
        .astype(jnp.bfloat16)
        .reshape(token_rows, head_number, VALUE_WIDTH)
    )
    d_prob = jnp.einsum(
        "qhv,khv->hqk", attended_gradient, values, preferred_element_type=jnp.float32
    )
    weights_wide = weights.astype(jnp.float32)
    delta = jnp.sum(weights_wide * d_prob, -1, keepdims=True)
    d_score = (weights_wide * (d_prob - delta) * score_scale).astype(jnp.bfloat16)
    dq_nope = jnp.einsum("hqk,khd->qhd", d_score, key_nope, preferred_element_type=jnp.float32)
    dq_rope = jnp.einsum("hqk,kd->qhd", d_score, rope_keys, preferred_element_type=jnp.float32)
    dq_rope = rotate(dq_rope, own_positions, -1.0)
    query_gradient = (
        jnp.concatenate([dq_nope, dq_rope], -1)
        .reshape(token_rows, head_number * per_head_width)
        .astype(jnp.bfloat16)
    )
    qb_term = contract_rows(query_rank_rows, query_gradient)
    query_adapter_gradient = lax.psum(
        columns_contract(query_gradient, query_adapter_second), "head"
    ).astype(jnp.bfloat16)
    qa_term = contract_rows(query_latent_rows, query_adapter_gradient)
    grad_qb, grad_qa = lax.psum((qb_term, qa_term), "ctx")
    return (grad_qa, grad_qb, grad_oa, grad_ob)


def solution(mesh):
    return jax.shard_map(
        body,
        mesh=mesh,
        in_specs=(
            P("ctx", "head"),
            P("ctx", None),
            P("ctx", None),
            P("ctx", None),
            P(None, "head"),
            P(),
            P(None, "head"),
            P("head", None),
            P(),
            P("head", "ctx"),
            P("ctx", None),
        ),
        out_specs=(P(), P(None, "head"), P("head", None), P(None, "ctx")),
        check_vma=False,
    )
```

profile of v0, /device:TPU:1, one launch (start us, length us, event | category | flops | bytes accessed | tf_op | source)
XLA Modules:
  0.0 902.7 jit_solution(16338640068785759681)
XLA Ops:
  7.3 8.5 collective-permute-start
  18.0 1.4 convolution_convert_fusion.7
  24.4 80.7 %all-gather = s32[64,1,2]{2,1,0:T(1,128)} all-gather(s32[1,1,2]{2,1,0:T(1,128)S(1)} %bitcast.209), channel_id=1, replica_groups=mesh['ctx'=64,'head'=8] {'ctx'}, dimensions={0}, use_global_device_ids=true | all-gather | bytes 520 | tf_op jit(solution)/shard_map/all_gather | solution.py:98
  123.5 2.0 fusion.62
  131.0 1.8 convolution_convert_fusion.8
  139.2 1.5 fusion.129
  140.7 1.4 copy.115
  143.5 1.9 concatenate.147
  145.4 1.9 constant_dynamic-update-slice_fusion.7
  148.7 1.9 concatenate.149
  150.6 2.0 constant_dynamic-update-slice_fusion.6
  152.6 1.9 collective-permute-start.1
  154.5 2.0 fusion.60
  156.5 10.0 %collective-permute-done.1 = bf16[128,576]{0,1:T(8,128)(2,1)S(1)} collective-permute-done((bf16[128,576]{0,1:T(8,128)(2,1)}, bf16[128,576]{0,1:T(8,128)(2,1)S(1)}, u32[]{:S(2)}, u32[]{:S(2)}) %collective-permute-start.1) | collective-permute-done | bytes 147488 | tf_op jit(solution)/shard_map/ppermute | solution.py:17
  168.2 1.9 collective-permute-start.2
  170.2 11.2 %collective-permute-done.2 = bf16[128,576]{0,1:T(8,128)(2,1)S(1)} collective-permute-done((bf16[128,576]{0,1:T(8,128)(2,1)S(1)}, bf16[128,576]{0,1:T(8,128)(2,1)S(1)}, u32[]{:S(2)}, u32[]{:S(2)}) %collective-permute-start.2) | collective-permute-done | bytes 147488 | tf_op jit(solution)/shard_map/ppermute | solution.py:17
  183.1 1.9 collective-permute-start.3
  185.0 11.9 %collective-permute-done.3 = bf16[128,576]{0,1:T(8,128)(2,1)S(1)} collective-permute-done((bf16[128,576]{0,1:T(8,128)(2,1)S(1)}, bf16[128,576]{0,1:T(8,128)(2,1)S(1)}, u32[]{:S(2)}, u32[]{:S(2)}) %collective-permute-start.3) | collective-permute-done | bytes 147488 | tf_op jit(solution)/shard_map/ppermute | solution.py:17
  199.9 1.4 copy.119
  201.3 1.4 copy.120
  207.0 1.9 concatenate.151
  208.9 1.9 concatenate.153
  210.7 1.9 concatenate.155
  212.6 1.9 collective-permute-start.4
  214.5 1.9 constant_dynamic-update-slice_fusion.5
  216.5 1.9 constant_dynamic-update-slice_fusion.4
  218.4 1.9 constant_dynamic-update-slice_fusion.3
  220.3 1.9 fusion.54
  222.3 3.1 collective-permute-done.4
  226.0 1.9 collective-permute-start.5
  228.9 10.8 %collective-permute-done.5 = bf16[128,576]{0,1:T(8,128)(2,1)S(1)} collective-permute-done((bf16[128,576]{0,1:T(8,128)(2,1)S(1)}, bf16[128,576]{0,1:T(8,128)(2,1)S(1)}, u32[]{:S(2)}, u32[]{:S(2)}) %collective-permute-start.5) | collective-permute-done | bytes 147488 | tf_op jit(solution)/shard_map/ppermute | solution.py:17
  240.4 1.9 collective-permute-start.6
  243.4 9.6 %collective-permute-done.6 = bf16[128,576]{0,1:T(8,128)(2,1)S(1)} collective-permute-done((bf16[128,576]{0,1:T(8,128)(2,1)S(1)}, bf16[128,576]{0,1:T(8,128)(2,1)S(1)}, u32[]{:S(2)}, u32[]{:S(2)}) %collective-permute-start.6) | collective-permute-done | bytes 147488 | tf_op jit(solution)/shard_map/ppermute | solution.py:17
  262.6 2.5 slice.337
  265.3 1.5 copy.186
  269.5 1.6 fusion.178
  271.0 1.9 fusion.188
  273.4 1.4 copy-done.18
  277.3 3.3 fusion.197
  280.9 2.7 fusion.16
  283.6 6.7 fusion.42
  290.4 7.4 fusion.43
  300.0 50.8 %all-reduce.2 = (bf16[128,32]{0,1:T(8,128)(2,1)S(1)}, bf16[128,32]{0,1:T(8,128)(2,1)S(1)}) all-reduce(f32[128,32]{0,1:T(8,128)S(1)} %fusion.200, f32[128,32]{0,1:T(8,128)} %fusion.201), channel_id=1, replica_groups=mesh['ctx'=64,'head'=8] {'head'}, use_global_device_ids=true, to_apply=%region_3.4 | all-reduce | flops 8192 | bytes 49152 | tf_op jit(solution)/shard_map/psum | solution.py:181
  354.6 535.1 %all-reduce.5.cloned.1.call-done = (f32[1536,32]{0,1:T(8,128)}, f32[32,1536]{1,0:T(8,128)}, f32[1024,32]{0,1:T(8,128)}, f32[32,2560]{1,0:T(8,128)}) async-done(((f32[1536,32]{0,1:T(8,128)}, f32[32,1536]{1,0:T(8,128)}, f32[1024,32]{0,1:T(8,128)}, f32[32,2560]{1,0:T(8,128)}), (f32[1536,32]{0,1:T(8,128)}, f32[32,1536]{1,0:T(8,128)}, f32[1024,32]{0,1:T(8,128)}, ...) | async-done | bytes 851984 | tf_op jit(solution)/shard_map/psum | solution.py:185
  889.6 1.4 constant_dynamic-slice_fusion.8
  891.1 1.6 copy.245
  892.7 1.6 copy.246
  894.3 1.6 copy.247
  (281 shorter events, 74.0 us)
Async XLA Ops:
  7.2 10.8 %copy-start = (bf16[512,2048]{1,0:T(8,128)(2,1)S(1)}, bf16[512,2048]{1,0:T(8,128)(2,1)}, u32[]{:S(2)}) copy-start(bf16[512,2048]{1,0:T(8,128)(2,1)} %param.15) | copy-start | bytes 6291460
  7.2 13.1 %copy-start.19 = (bf16[128,1536]{1,0:T(8,128)(2,1)S(1)}, bf16[128,1536]{1,0:T(8,128)(2,1)}, u32[]{:S(2)}) copy-start(bf16[128,1536]{1,0:T(8,128)(2,1)} %param.12) | copy-start | bytes 1179652
  7.2 14.0 %copy-start.21 = (bf16[128,1536]{1,0:T(8,128)(2,1)S(1)}, bf16[128,1536]{1,0:T(8,128)(2,1)}, u32[]{:S(2)}) copy-start(bf16[128,1536]{1,0:T(8,128)(2,1)} %param.11) | copy-start | bytes 1179652
  7.2 16.6 %copy-start.62 = (s32[1,2]{1,0:T(1,128)S(1)}, s32[1,2]{1,0:T(1,128)}, u32[]{:S(2)}) copy-start(s32[1,2]{1,0:T(1,128)} %param.14) | copy-start | bytes 28
  7.2 270.1 %all-gather.3.cloned.1.call-start = ((), (), s32[]{:S(2)}) async-start(), calls=%async_computation | async-start | bytes 5324800 | tf_op jit(solution)/shard_map/all_gather | solution.py:159
  7.3 128.1 %collective-permute-start = (bf16[128,576]{0,1:T(8,128)(2,1)}, bf16[128,576]{0,1:T(8,128)(2,1)}, u32[]{:S(2)}, u32[]{:S(2)}) collective-permute-start(bf16[128,576]{0,1:T(8,128)(2,1)} %param.13), channel_id=1, source_target_pairs={{0,64},{8,72},{16,80},{24,88},{32,96},{40,104},{48,112},{56,120},{... | collective-permute-start | bytes 442376 | tf_op jit(solution)/shard_map/ppermute | solution.py:17
  15.8 873.8 %all-reduce.5.cloned.1.call-start = ((), (), s32[]{:S(2)}) async-start(), calls=%async_computation.1 | async-start | bytes 1703936 | tf_op jit(solution)/shard_map/psum | solution.py:185
  16.0 4.3 copy-start.28
  16.0 5.1 copy-start.22
  18.0 113.1 %copy-start.2 = (bf16[128,2560]{1,0:T(8,128)(2,1)S(1)}, bf16[128,2560]{1,0:T(8,128)(2,1)}, u32[]{:S(2)}) copy-start(bf16[128,2560]{1,0:T(8,128)(2,1)} %param.21) | copy-start | bytes 1966084
  109.0 19.7 %copy-start.70 = (s32[64]{0:T(128)}, s32[64]{0:T(128)S(1)}, u32[]{:S(2)}) copy-start(s32[64]{0:T(128)S(1)} %iota_add_fusion.14) | copy-start | bytes 772
  109.6 19.1 %copy-start.71 = (s32[64]{0:T(128)}, s32[64]{0:T(128)S(1)}, u32[]{:S(2)}) copy-start(s32[64]{0:T(128)S(1)} %iota_add_fusion.15) | copy-start | bytes 772
  110.9 17.8 %copy-start.78 = (s32[64]{0:T(128)}, s32[64]{0:T(128)S(1)}, u32[]{:S(2)}) copy-start(s32[64]{0:T(128)S(1)} %iota_add_fusion.2) | copy-start | bytes 772
  111.5 17.2 %copy-start.79 = (s32[64]{0:T(128)}, s32[64]{0:T(128)S(1)}, u32[]{:S(2)}) copy-start(s32[64]{0:T(128)S(1)} %iota_add_fusion.3) | copy-start | bytes 772
  112.8 15.9 %copy-start.72 = (s32[64]{0:T(128)}, s32[64]{0:T(128)S(1)}, u32[]{:S(2)}) copy-start(s32[64]{0:T(128)S(1)} %iota_add_fusion.6) | copy-start | bytes 772
  113.5 15.3 %copy-start.73 = (s32[64]{0:T(128)}, s32[64]{0:T(128)S(1)}, u32[]{:S(2)}) copy-start(s32[64]{0:T(128)S(1)} %iota_add_fusion.7) | copy-start | bytes 772
  114.7 14.0 %copy-start.74 = (s32[64]{0:T(128)}, s32[64]{0:T(128)S(1)}, u32[]{:S(2)}) copy-start(s32[64]{0:T(128)S(1)} %iota_add_fusion.4) | copy-start | bytes 772
  115.4 13.4 %copy-start.75 = (s32[64]{0:T(128)}, s32[64]{0:T(128)S(1)}, u32[]{:S(2)}) copy-start(s32[64]{0:T(128)S(1)} %iota_add_fusion.5) | copy-start | bytes 772
  130.2 9.0 %copy-start.26 = (f32[128,64]{0,1:T(8,128)S(1)}, f32[128,64]{0,1:T(8,128)}, u32[]{:S(2)}) copy-start(f32[128,64]{0,1:T(8,128)} %slice_convert_fusion.8) | copy-start | bytes 98308
  130.2 9.0 %copy-start.68 = (f32[128]{0:T(128)S(1)}, f32[128]{0:T(128)}, u32[]{:S(2)}) copy-start(f32[128]{0:T(128)} %get-tuple-element.77) | copy-start | bytes 1540
  130.2 9.0 %copy-start.69 = (f32[128]{0:T(128)S(1)}, f32[128]{0:T(128)}, u32[]{:S(2)}) copy-start(f32[128]{0:T(128)} %get-tuple-element.78) | copy-start | bytes 1540
  140.7 26.3 %copy-start.32 = (bf16[128,32]{0,1:T(8,128)(2,1)}, bf16[128,32]{0,1:T(8,128)(2,1)S(1)}, u32[]{:S(2)}) copy-start(bf16[128,32]{0,1:T(8,128)(2,1)S(1)} %get-tuple-element.30) | copy-start | bytes 24580
  140.7 26.3 %copy-start.34 = (bf16[128,32]{0,1:T(8,128)(2,1)}, bf16[128,32]{0,1:T(8,128)(2,1)S(1)}, u32[]{:S(2)}) copy-start(bf16[128,32]{0,1:T(8,128)(2,1)S(1)} %get-tuple-element.31) | copy-start | bytes 24580
  152.6 13.9 %collective-permute-start.1 = (bf16[128,576]{0,1:T(8,128)(2,1)}, bf16[128,576]{0,1:T(8,128)(2,1)S(1)}, u32[]{:S(2)}, u32[]{:S(2)}) collective-permute-start(bf16[128,576]{0,1:T(8,128)(2,1)} %collective-permute-done), channel_id=1, source_target_pairs={{0,64},{8,72},{16,80},{24,88},{32,96},{40,104},{48,112},{56,120},{... | collective-permute-start | bytes 442376 | tf_op jit(solution)/shard_map/ppermute | solution.py:17
  167.0 16.1 %copy-start.5 = (bf16[128,2048]{1,0:T(8,128)(2,1)}, bf16[128,2048]{1,0:T(8,128)(2,1)S(1)}, u32[]{:S(2)}) copy-start(bf16[128,2048]{1,0:T(8,128)(2,1)S(1)} %convolution_convert_fusion.5) | copy-start | bytes 1572868
  168.2 13.1 %collective-permute-start.2 = (bf16[128,576]{0,1:T(8,128)(2,1)S(1)}, bf16[128,576]{0,1:T(8,128)(2,1)S(1)}, u32[]{:S(2)}, u32[]{:S(2)}) collective-permute-start(bf16[128,576]{0,1:T(8,128)(2,1)S(1)} %collective-permute-done.1), channel_id=1, source_target_pairs={{0,64},{8,72},{16,80},{24,88},{32,96},{40,104},{48,112},{56,120},{... | collective-permute-start | bytes 442376 | tf_op jit(solution)/shard_map/ppermute | solution.py:17
  181.8 17.1 %copy-start.60 = (f32[32]{0:T(128)S(1)}, f32[32]{0:T(128)}, u32[]{:S(2)}) copy-start(f32[32]{0:T(128)} %multiply_power_fusion) | copy-start | bytes 388
  181.8 17.1 %copy-start.66 = (f32[128]{0:T(128)S(1)}, f32[128]{0:T(128)}, u32[]{:S(2)}) copy-start(f32[128]{0:T(128)} %get-tuple-element.79) | copy-start | bytes 1540
  181.8 17.1 %copy-start.67 = (f32[128]{0:T(128)S(1)}, f32[128]{0:T(128)}, u32[]{:S(2)}) copy-start(f32[128]{0:T(128)} %get-tuple-element.80) | copy-start | bytes 1540
  181.9 17.1 %copy-start.77 = (f32[128]{0:T(128)S(1)}, f32[128]{0:T(128)}, u32[]{:S(2)}) copy-start(f32[128]{0:T(128)} %add_convert_fusion.6) | copy-start | bytes 1540
  183.1 13.8 %collective-permute-start.3 = (bf16[128,576]{0,1:T(8,128)(2,1)S(1)}, bf16[128,576]{0,1:T(8,128)(2,1)S(1)}, u32[]{:S(2)}, u32[]{:S(2)}) collective-permute-start(bf16[128,576]{0,1:T(8,128)(2,1)S(1)} %collective-permute-done.2), channel_id=1, source_target_pairs={{0,64},{8,72},{16,80},{24,88},{32,96},{40,104},{48,112},{56,120},{... | collective-permute-start | bytes 442376 | tf_op jit(solution)/shard_map/ppermute | solution.py:17
  199.9 25.9 %copy-start.38 = (bf16[128,32]{0,1:T(8,128)(2,1)}, bf16[128,32]{0,1:T(8,128)(2,1)S(1)}, u32[]{:S(2)}) copy-start(bf16[128,32]{0,1:T(8,128)(2,1)S(1)} %get-tuple-element.24) | copy-start | bytes 24580
  199.9 25.9 %copy-start.40 = (bf16[128,32]{0,1:T(8,128)(2,1)}, bf16[128,32]{0,1:T(8,128)(2,1)S(1)}, u32[]{:S(2)}) copy-start(bf16[128,32]{0,1:T(8,128)(2,1)S(1)} %get-tuple-element.25) | copy-start | bytes 24580
  212.6 12.7 %collective-permute-start.4 = (bf16[128,576]{0,1:T(8,128)(2,1)}, bf16[128,576]{0,1:T(8,128)(2,1)S(1)}, u32[]{:S(2)}, u32[]{:S(2)}) collective-permute-start(bf16[128,576]{0,1:T(8,128)(2,1)} %copy-done.25), channel_id=1, source_target_pairs={{0,64},{8,72},{16,80},{24,88},{32,96},{40,104},{48,112},{56,120},{... | collective-permute-start | bytes 442376 | tf_op jit(solution)/shard_map/ppermute | solution.py:17
  225.8 17.6 %copy-start.4 = (bf16[128,2048]{1,0:T(8,128)(2,1)}, bf16[128,2048]{1,0:T(8,128)(2,1)S(1)}, u32[]{:S(2)}) copy-start(bf16[128,2048]{1,0:T(8,128)(2,1)S(1)} %convolution_convert_fusion.2) | copy-start | bytes 1572868
  226.0 13.8 %collective-permute-start.5 = (bf16[128,576]{0,1:T(8,128)(2,1)S(1)}, bf16[128,576]{0,1:T(8,128)(2,1)S(1)}, u32[]{:S(2)}, u32[]{:S(2)}) collective-permute-start(bf16[128,576]{0,1:T(8,128)(2,1)S(1)} %collective-permute-done.4), channel_id=1, source_target_pairs={{0,64},{8,72},{16,80},{24,88},{32,96},{40,104},{48,112},{56,120},{... | collective-permute-start | bytes 442376 | tf_op jit(solution)/shard_map/ppermute | solution.py:17
  240.2 14.2 %copy-start.61 = (f32[32]{0:T(128)S(1)}, f32[32]{0:T(128)}, u32[]{:S(2)}) copy-start(f32[32]{0:T(128)} %multiply_power_fusion) | copy-start | bytes 388
  240.2 14.2 %copy-start.63 = (f32[128]{0:T(128)S(1)}, f32[128]{0:T(128)}, u32[]{:S(2)}) copy-start(f32[128]{0:T(128)} %get-tuple-element.10) | copy-start | bytes 1540
  240.3 14.2 %copy-start.64 = (f32[128]{0:T(128)S(1)}, f32[128]{0:T(128)}, u32[]{:S(2)}) copy-start(f32[128]{0:T(128)} %get-tuple-element.81) | copy-start | bytes 1540
  240.3 14.2 %copy-start.65 = (f32[128]{0:T(128)S(1)}, f32[128]{0:T(128)}, u32[]{:S(2)}) copy-start(f32[128]{0:T(128)} %get-tuple-element.82) | copy-start | bytes 1540
  240.3 14.2 %copy-start.76 = (f32[128]{0:T(128)S(1)}, f32[128]{0:T(128)}, u32[]{:S(2)}) copy-start(f32[128]{0:T(128)} %add_convert_fusion.9) | copy-start | bytes 1540
  240.4 12.6 %collective-permute-start.6 = (bf16[128,576]{0,1:T(8,128)(2,1)S(1)}, bf16[128,576]{0,1:T(8,128)(2,1)S(1)}, u32[]{:S(2)}, u32[]{:S(2)}) collective-permute-start(bf16[128,576]{0,1:T(8,128)(2,1)S(1)} %collective-permute-done.5), channel_id=1, source_target_pairs={{0,64},{8,72},{16,80},{24,88},{32,96},{40,104},{48,112},{56,120},{... | collective-permute-start | bytes 442376 | tf_op jit(solution)/shard_map/ppermute | solution.py:17
  273.0 3.5 copy-start.31
  290.4 7.5 copy-start.58
  290.4 8.5 copy-start.23
  290.4 8.7 copy-start.30
  290.4 60.4 %copy-start.20 = (bf16[128,1536]{1,0:T(8,128)(2,1)S(1)}, bf16[128,1536]{1,0:T(8,128)(2,1)}, u32[]{:S(2)}) copy-start(bf16[128,1536]{1,0:T(8,128)(2,1)} %param.12) | copy-start | bytes 1179652
  290.4 605.5 %copy-start.1 = (bf16[512,2048]{1,0:T(8,128)(2,1)S(1)}, bf16[512,2048]{1,0:T(8,128)(2,1)}, u32[]{:S(2)}) copy-start(bf16[512,2048]{1,0:T(8,128)(2,1)} %param.15) | copy-start | bytes 6291460
  (41 other events, 68.4 us)
Sparse Core Ops, SparseCore 0:
  15.9 122.1 all-gather.2
  352.8 536.8 all-reduce.4
where the time goes:
time: 905 us; the launch traced here: 903 us
  waiting for transfers between devices  592 us (65%)
  blocking collectives  131 us (14%)
  local copies, waits for them, and re-layouts  66.2 us (7%)
  matrix products  47 us (5%)
  other arithmetic  30 us (3%)
  starting transfers between devices  20.1 us (2%)
  between operations  16.3 us (2%)
    psum x1, waiting for transfers between devices, body(): grad_qb, grad_qa = lax.psum((qb_term, qa_term), 'ctx')  535 us
    all_gather x1, blocking collectives, body(): all_offsets = lax.all_gather(block_starts, 'ctx', axis=0, tiled=True)  80.7 us
    ppermute x7, waiting for transfers between devices, passed_along(): return lax.ppermute(value, axis, pairs)  56.6 us
    psum x1, blocking collectives, body(): lax.psum(columns_contract(query_gradient, query_adapter_second), 'head')  50.8 us
    unnamed x181, local copies, waits for them, and re-layouts  26.2 us
    ppermute x7, starting transfers between devices, passed_along(): return lax.ppermute(value, axis, pairs)  20 us
  transfers between devices with their start and end apart: 9, of which 7 were waited for; matrix products, arithmetic and copies ran while one was open for 12% of the time, Pallas kernels for 0%

commit v1 on v0

--- a/solution.py
+++ b/solution.py
@@ -95,7 +95,15 @@
     axis_count = lax.axis_size("ctx")
     stride = axis_count // SPAN
     axis_place = lax.axis_index("ctx")
-    all_offsets = lax.all_gather(block_starts, "ctx", axis=0, tiled=True)
+    all_offsets = jnp.concatenate(
+        lax.all_to_all(
+            jnp.stack([block_starts for _ in range(lax.axis_size("ctx"))]),
+            axis_name="ctx",
+            split_axis=0,
+            concat_axis=0,
+        ),
+        axis=0,
+    )
     own_positions = block_positions(block_starts[0], half_rows)
     query_rank_rows = jnp.dot(
         query_latent_rows, query_adapter_first, preferred_element_type=jnp.float32

time: 905 us -> 841 us (0.929)
  blocking collectives: 131 us -> 44.9 us
  starting transfers between devices: 20.1 us -> 38.6 us
    all_gather x1 -> x0, blocking collectives: 80.7 us -> none  [body(): all_offsets = lax.all_gather(block_starts, 'ctx', axis=0, tiled=True)]
    all_to_all x0 -> x1, starting transfers between devices: none -> 11.1 us  [body(): lax.all_to_all(jnp.stack([block_starts for _ in range(lax.axis_size('ctx'...]
    unnamed x181 -> x175, local copies, waits for them, and re-layouts: 26.2 us -> 26.2 us
  transfers between devices with their start and end apart: 9 -> 10, of which waited for: 7 -> 7; matrix products, arithmetic and copies ran while one was open for 12% -> 13% of each run, Pallas kernels for 0% -> 0%
where the time goes in v1:
time: 841 us; the launch traced here: 839 us
  waiting for transfers between devices  591 us (70%)
  local copies, waits for them, and re-layouts  68.1 us (8%)
  matrix products  49.5 us (6%)
  blocking collectives  44.9 us (5%)
  starting transfers between devices  38.6 us (5%)
  other arithmetic  29.8 us (4%)
  between operations  16.3 us (2%)
    psum x1, waiting for transfers between devices, body(): grad_qb, grad_qa = lax.psum((qb_term, qa_term), 'ctx')  539 us
    ppermute x7, waiting for transfers between devices, passed_along(): return lax.ppermute(value, axis, pairs)  52 us
    psum x1, blocking collectives, body(): lax.psum(columns_contract(query_gradient, query_adapter_second), 'head')  44.9 us
    ppermute x7, starting transfers between devices, passed_along(): return lax.ppermute(value, axis, pairs)  27.4 us
    unnamed x175, local copies, waits for them, and re-layouts  26.2 us
  transfers between devices with their start and end apart: 10, of which 7 were waited for; matrix products, arithmetic and copies ran while one was open for 13% of the time, Pallas kernels for 0%

profile of v1, /device:TPU:1, one launch (start us, length us, event | category | flops | bytes accessed | tf_op | source)
XLA Modules:
  0.0 838.7 jit_solution(392956998926886347)
XLA Ops:
  7.2 8.4 %collective-permute-start = (bf16[128,576]{0,1:T(8,128)(2,1)}, bf16[128,576]{0,1:T(8,128)(2,1)}, u32[]{:S(2)}, u32[]{:S(2)}) collective-permute-start(bf16[128,576]{0,1:T(8,128)(2,1)} %param.13), channel_id=1, source_target_pairs={{0,64},{8,72},{16,80},{24,88},{32,96},{40,104},{48,112},{56,120},{... | collective-permute-start | bytes 442376 | tf_op jit(solution)/shard_map/ppermute | solution.py:17
  16.9 11.1 %all-to-all-start = ((s32[64,1,2]{2,1,0:T(1,128)}), s32[64,1,2]{2,1,0:T(1,128)}, u32[]{:S(2)}, u32[]{:S(2)}) async-start(s32[64,1,2]{2,1,0:T(1,128)} %stack.2), calls=%async_computation | async-start | bytes 65536 | tf_op jit(solution)/shard_map/all_to_all | solution.py:99
  32.2 1.4 convolution_convert_fusion.7
  38.0 2.0 fusion.62
  41.9 1.8 convolution_convert_fusion.8
  72.1 1.4 fusion.129
  73.5 1.4 copy.115
  76.4 1.9 concatenate.147
  78.2 1.9 constant_dynamic-update-slice_fusion.7
  81.6 1.9 concatenate.149
  83.4 2.0 constant_dynamic-update-slice_fusion.6
  85.4 7.1 collective-permute-start.1
  92.6 2.0 fusion.60
  94.5 8.1 collective-permute-done.1
  104.3 4.2 collective-permute-start.2
  108.6 9.9 %collective-permute-done.2 = bf16[128,576]{0,1:T(8,128)(2,1)S(1)} collective-permute-done((bf16[128,576]{0,1:T(8,128)(2,1)S(1)}, bf16[128,576]{0,1:T(8,128)(2,1)S(1)}, u32[]{:S(2)}, u32[]{:S(2)}) %collective-permute-start.2) | collective-permute-done | bytes 147488 | tf_op jit(solution)/shard_map/ppermute | solution.py:17
  120.2 1.9 collective-permute-start.3
  122.1 10.9 %collective-permute-done.3 = bf16[128,576]{0,1:T(8,128)(2,1)S(1)} collective-permute-done((bf16[128,576]{0,1:T(8,128)(2,1)S(1)}, bf16[128,576]{0,1:T(8,128)(2,1)S(1)}, u32[]{:S(2)}, u32[]{:S(2)}) %collective-permute-start.3) | collective-permute-done | bytes 147488 | tf_op jit(solution)/shard_map/ppermute | solution.py:17
  136.0 1.4 copy.119
  143.1 1.9 concatenate.151
  144.9 1.9 concatenate.153
  146.8 1.9 concatenate.155
  148.7 1.9 collective-permute-start.4
  150.6 1.9 constant_dynamic-update-slice_fusion.5
  152.6 1.9 constant_dynamic-update-slice_fusion.4
  154.5 1.9 constant_dynamic-update-slice_fusion.3
  156.4 1.9 fusion.54
  158.3 3.3 collective-permute-done.4
  162.3 1.9 collective-permute-start.5
  165.2 9.6 %collective-permute-done.5 = bf16[128,576]{0,1:T(8,128)(2,1)S(1)} collective-permute-done((bf16[128,576]{0,1:T(8,128)(2,1)S(1)}, bf16[128,576]{0,1:T(8,128)(2,1)S(1)}, u32[]{:S(2)}, u32[]{:S(2)}) %collective-permute-start.5) | collective-permute-done | bytes 147488 | tf_op jit(solution)/shard_map/ppermute | solution.py:17
  175.4 1.9 collective-permute-start.6
  178.4 10.3 %collective-permute-done.6 = bf16[128,576]{0,1:T(8,128)(2,1)S(1)} collective-permute-done((bf16[128,576]{0,1:T(8,128)(2,1)S(1)}, bf16[128,576]{0,1:T(8,128)(2,1)S(1)}, u32[]{:S(2)}, u32[]{:S(2)}) %collective-permute-start.6) | collective-permute-done | bytes 147488 | tf_op jit(solution)/shard_map/ppermute | solution.py:17
  198.3 2.5 slice.337
  201.0 1.5 copy.186
  205.1 1.6 fusion.170
  206.7 1.9 fusion.180
  209.1 1.4 copy-done.18
  213.0 3.3 fusion.189
  217.5 2.7 fusion.16
  220.2 6.0 fusion.42
  226.2 8.2 fusion.43
  236.5 1.6 fusion.190
  238.1 44.9 %all-reduce.2 = (bf16[128,32]{0,1:T(8,128)(2,1)S(1)}, bf16[128,32]{0,1:T(8,128)(2,1)S(1)}) all-reduce(f32[128,32]{0,1:T(8,128)S(1)} %fusion.192, f32[128,32]{0,1:T(8,128)} %fusion.193), channel_id=1, replica_groups=mesh['ctx'=64,'head'=8] {'head'}, use_global_device_ids=true, to_apply=%region_3.4 | all-reduce | flops 8192 | bytes 49152 | tf_op jit(solution)/shard_map/psum | solution.py:189
  286.8 538.8 %all-reduce.5.cloned.1.call-done = (f32[1536,32]{0,1:T(8,128)}, f32[32,1536]{1,0:T(8,128)}, f32[1024,32]{0,1:T(8,128)}, f32[32,2560]{1,0:T(8,128)}) async-done(((f32[1536,32]{0,1:T(8,128)}, f32[32,1536]{1,0:T(8,128)}, f32[1024,32]{0,1:T(8,128)}, f32[32,2560]{1,0:T(8,128)}), (f32[1536,32]{0,1:T(8,128)}, f32[32,1536]{1,0:T(8,128)}, f32[1024,32]{0,1:T(8,128)}, ...) | async-done | bytes 851984 | tf_op jit(solution)/shard_map/psum | solution.py:193
  825.6 1.4 constant_dynamic-slice_fusion.8
  827.0 1.6 copy.245
  828.7 1.6 copy.246
  830.3 1.6 copy.247
  (277 shorter events, 78.7 us)
Async XLA Ops:
  7.2 25.0 %copy-start = (bf16[512,2048]{1,0:T(8,128)(2,1)S(1)}, bf16[512,2048]{1,0:T(8,128)(2,1)}, u32[]{:S(2)}) copy-start(bf16[512,2048]{1,0:T(8,128)(2,1)} %param.15) | copy-start | bytes 6291460
  7.2 27.3 %copy-start.27 = (bf16[1536,32]{0,1:T(8,128)(2,1)S(1)}, bf16[1536,32]{0,1:T(8,128)(2,1)}, u32[]{:S(2)}) copy-start(bf16[1536,32]{0,1:T(8,128)(2,1)} %param.16) | copy-start | bytes 294916
  7.2 28.2 %copy-start.22 = (bf16[32,1536]{1,0:T(8,128)(2,1)S(1)}, bf16[32,1536]{1,0:T(8,128)(2,1)}, u32[]{:S(2)}) copy-start(bf16[32,1536]{1,0:T(8,128)(2,1)} %param.17) | copy-start | bytes 294916
  7.2 61.0 %collective-permute-start = (bf16[128,576]{0,1:T(8,128)(2,1)}, bf16[128,576]{0,1:T(8,128)(2,1)}, u32[]{:S(2)}, u32[]{:S(2)}) collective-permute-start(bf16[128,576]{0,1:T(8,128)(2,1)} %param.13), channel_id=1, source_target_pairs={{0,64},{8,72},{16,80},{24,88},{32,96},{40,104},{48,112},{56,120},{... | collective-permute-start | bytes 442376 | tf_op jit(solution)/shard_map/ppermute | solution.py:17
  16.9 26.8 %all-to-all-start = ((s32[64,1,2]{2,1,0:T(1,128)}), s32[64,1,2]{2,1,0:T(1,128)}, u32[]{:S(2)}, u32[]{:S(2)}) async-start(s32[64,1,2]{2,1,0:T(1,128)} %stack.2), calls=%async_computation | async-start | bytes 65536 | tf_op jit(solution)/shard_map/all_to_all | solution.py:99
  28.0 185.0 %all-gather.2.cloned.1.call-start = ((), (), s32[]{:S(2)}) async-start(), calls=%async_computation.1 | async-start | bytes 5324800 | tf_op jit(solution)/shard_map/all_gather | solution.py:167
  28.8 796.8 %all-reduce.5.cloned.1.call-start = ((), (), s32[]{:S(2)}) async-start(), calls=%async_computation.2 | async-start | bytes 1703936 | tf_op jit(solution)/shard_map/psum | solution.py:193
  29.0 5.6 copy-start.19
  29.0 6.4 copy-start.21
  32.2 9.7 %copy-start.2 = (bf16[128,2560]{1,0:T(8,128)(2,1)S(1)}, bf16[128,2560]{1,0:T(8,128)(2,1)}, u32[]{:S(2)}) copy-start(bf16[128,2560]{1,0:T(8,128)(2,1)} %param.21) | copy-start | bytes 1966084
  47.5 15.8 %copy-start.67 = (s32[64]{0:T(128)}, s32[64]{0:T(128)S(1)}, u32[]{:S(2)}) copy-start(s32[64]{0:T(128)S(1)} %iota_add_fusion.14) | copy-start | bytes 772
  48.2 15.1 %copy-start.68 = (s32[64]{0:T(128)}, s32[64]{0:T(128)S(1)}, u32[]{:S(2)}) copy-start(s32[64]{0:T(128)S(1)} %iota_add_fusion.15) | copy-start | bytes 772
  49.5 13.9 %copy-start.75 = (s32[64]{0:T(128)}, s32[64]{0:T(128)S(1)}, u32[]{:S(2)}) copy-start(s32[64]{0:T(128)S(1)} %iota_add_fusion.2) | copy-start | bytes 772
  50.1 13.2 %copy-start.76 = (s32[64]{0:T(128)}, s32[64]{0:T(128)S(1)}, u32[]{:S(2)}) copy-start(s32[64]{0:T(128)S(1)} %iota_add_fusion.3) | copy-start | bytes 772
  51.4 12.0 %copy-start.69 = (s32[64]{0:T(128)}, s32[64]{0:T(128)S(1)}, u32[]{:S(2)}) copy-start(s32[64]{0:T(128)S(1)} %iota_add_fusion.6) | copy-start | bytes 772
  52.0 11.3 %copy-start.70 = (s32[64]{0:T(128)}, s32[64]{0:T(128)S(1)}, u32[]{:S(2)}) copy-start(s32[64]{0:T(128)S(1)} %iota_add_fusion.7) | copy-start | bytes 772
  53.3 10.1 %copy-start.71 = (s32[64]{0:T(128)}, s32[64]{0:T(128)S(1)}, u32[]{:S(2)}) copy-start(s32[64]{0:T(128)S(1)} %iota_add_fusion.4) | copy-start | bytes 772
  54.0 9.4 %copy-start.72 = (s32[64]{0:T(128)}, s32[64]{0:T(128)S(1)}, u32[]{:S(2)}) copy-start(s32[64]{0:T(128)S(1)} %iota_add_fusion.5) | copy-start | bytes 772
  64.9 7.2 copy-start.25
  64.9 7.2 copy-start.65
  64.9 7.2 copy-start.66
  73.5 29.5 %copy-start.30 = (bf16[128,32]{0,1:T(8,128)(2,1)}, bf16[128,32]{0,1:T(8,128)(2,1)S(1)}, u32[]{:S(2)}) copy-start(bf16[128,32]{0,1:T(8,128)(2,1)S(1)} %get-tuple-element.30) | copy-start | bytes 24580
  73.5 29.6 %copy-start.32 = (bf16[128,32]{0,1:T(8,128)(2,1)}, bf16[128,32]{0,1:T(8,128)(2,1)S(1)}, u32[]{:S(2)}) copy-start(bf16[128,32]{0,1:T(8,128)(2,1)S(1)} %get-tuple-element.31) | copy-start | bytes 24580
  85.4 17.2 %collective-permute-start.1 = (bf16[128,576]{0,1:T(8,128)(2,1)}, bf16[128,576]{0,1:T(8,128)(2,1)S(1)}, u32[]{:S(2)}, u32[]{:S(2)}) collective-permute-start(bf16[128,576]{0,1:T(8,128)(2,1)} %collective-permute-done), channel_id=1, source_target_pairs={{0,64},{8,72},{16,80},{24,88},{32,96},{40,104},{48,112},{56,120},{... | collective-permute-start | bytes 442376 | tf_op jit(solution)/shard_map/ppermute | solution.py:17
  103.1 17.1 %copy-start.5 = (bf16[128,2048]{1,0:T(8,128)(2,1)}, bf16[128,2048]{1,0:T(8,128)(2,1)S(1)}, u32[]{:S(2)}) copy-start(bf16[128,2048]{1,0:T(8,128)(2,1)S(1)} %convolution_convert_fusion.5) | copy-start | bytes 1572868
  104.3 14.2 %collective-permute-start.2 = (bf16[128,576]{0,1:T(8,128)(2,1)S(1)}, bf16[128,576]{0,1:T(8,128)(2,1)S(1)}, u32[]{:S(2)}, u32[]{:S(2)}) collective-permute-start(bf16[128,576]{0,1:T(8,128)(2,1)S(1)} %collective-permute-done.1), channel_id=1, source_target_pairs={{0,64},{8,72},{16,80},{24,88},{32,96},{40,104},{48,112},{56,120},{... | collective-permute-start | bytes 442376 | tf_op jit(solution)/shard_map/ppermute | solution.py:17
  119.0 3.2 copy-start.7
  119.0 16.2 %copy-start.58 = (f32[32]{0:T(128)S(1)}, f32[32]{0:T(128)}, u32[]{:S(2)}) copy-start(f32[32]{0:T(128)} %multiply_power_fusion) | copy-start | bytes 388
  119.0 16.1 %copy-start.63 = (f32[128]{0:T(128)S(1)}, f32[128]{0:T(128)}, u32[]{:S(2)}) copy-start(f32[128]{0:T(128)} %get-tuple-element.79) | copy-start | bytes 1540
  119.0 16.1 %copy-start.64 = (f32[128]{0:T(128)S(1)}, f32[128]{0:T(128)}, u32[]{:S(2)}) copy-start(f32[128]{0:T(128)} %get-tuple-element.80) | copy-start | bytes 1540
  119.0 16.1 %copy-start.74 = (f32[128]{0:T(128)S(1)}, f32[128]{0:T(128)}, u32[]{:S(2)}) copy-start(f32[128]{0:T(128)} %add_convert_fusion.6) | copy-start | bytes 1540
  120.2 12.8 %collective-permute-start.3 = (bf16[128,576]{0,1:T(8,128)(2,1)S(1)}, bf16[128,576]{0,1:T(8,128)(2,1)S(1)}, u32[]{:S(2)}, u32[]{:S(2)}) collective-permute-start(bf16[128,576]{0,1:T(8,128)(2,1)S(1)} %collective-permute-done.2), channel_id=1, source_target_pairs={{0,64},{8,72},{16,80},{24,88},{32,96},{40,104},{48,112},{56,120},{... | collective-permute-start | bytes 442376 | tf_op jit(solution)/shard_map/ppermute | solution.py:17
  136.0 26.1 %copy-start.36 = (bf16[128,32]{0,1:T(8,128)(2,1)}, bf16[128,32]{0,1:T(8,128)(2,1)S(1)}, u32[]{:S(2)}) copy-start(bf16[128,32]{0,1:T(8,128)(2,1)S(1)} %get-tuple-element.24) | copy-start | bytes 24580
  136.0 26.1 %copy-start.38 = (bf16[128,32]{0,1:T(8,128)(2,1)}, bf16[128,32]{0,1:T(8,128)(2,1)S(1)}, u32[]{:S(2)}) copy-start(bf16[128,32]{0,1:T(8,128)(2,1)S(1)} %get-tuple-element.25) | copy-start | bytes 24580
  148.7 12.9 %collective-permute-start.4 = (bf16[128,576]{0,1:T(8,128)(2,1)}, bf16[128,576]{0,1:T(8,128)(2,1)S(1)}, u32[]{:S(2)}, u32[]{:S(2)}) collective-permute-start(bf16[128,576]{0,1:T(8,128)(2,1)} %copy-done.24), channel_id=1, source_target_pairs={{0,64},{8,72},{16,80},{24,88},{32,96},{40,104},{48,112},{56,120},{... | collective-permute-start | bytes 442376 | tf_op jit(solution)/shard_map/ppermute | solution.py:17
  162.1 16.3 %copy-start.4 = (bf16[128,2048]{1,0:T(8,128)(2,1)}, bf16[128,2048]{1,0:T(8,128)(2,1)S(1)}, u32[]{:S(2)}) copy-start(bf16[128,2048]{1,0:T(8,128)(2,1)S(1)} %convolution_convert_fusion.2) | copy-start | bytes 1572868
  162.3 12.5 %collective-permute-start.5 = (bf16[128,576]{0,1:T(8,128)(2,1)S(1)}, bf16[128,576]{0,1:T(8,128)(2,1)S(1)}, u32[]{:S(2)}, u32[]{:S(2)}) collective-permute-start(bf16[128,576]{0,1:T(8,128)(2,1)S(1)} %collective-permute-done.4), channel_id=1, source_target_pairs={{0,64},{8,72},{16,80},{24,88},{32,96},{40,104},{48,112},{56,120},{... | collective-permute-start | bytes 442376 | tf_op jit(solution)/shard_map/ppermute | solution.py:17
  175.2 3.2 copy-start.6
  175.2 14.9 %copy-start.59 = (f32[32]{0:T(128)S(1)}, f32[32]{0:T(128)}, u32[]{:S(2)}) copy-start(f32[32]{0:T(128)} %multiply_power_fusion) | copy-start | bytes 388
  175.3 14.9 %copy-start.60 = (f32[128]{0:T(128)S(1)}, f32[128]{0:T(128)}, u32[]{:S(2)}) copy-start(f32[128]{0:T(128)} %get-tuple-element.10) | copy-start | bytes 1540
  175.3 14.9 %copy-start.61 = (f32[128]{0:T(128)S(1)}, f32[128]{0:T(128)}, u32[]{:S(2)}) copy-start(f32[128]{0:T(128)} %get-tuple-element.81) | copy-start | bytes 1540
  175.3 14.9 %copy-start.62 = (f32[128]{0:T(128)S(1)}, f32[128]{0:T(128)}, u32[]{:S(2)}) copy-start(f32[128]{0:T(128)} %get-tuple-element.82) | copy-start | bytes 1540
  175.3 14.9 %copy-start.73 = (f32[128]{0:T(128)S(1)}, f32[128]{0:T(128)}, u32[]{:S(2)}) copy-start(f32[128]{0:T(128)} %add_convert_fusion.9) | copy-start | bytes 1540
  175.4 13.3 %collective-permute-start.6 = (bf16[128,576]{0,1:T(8,128)(2,1)S(1)}, bf16[128,576]{0,1:T(8,128)(2,1)S(1)}, u32[]{:S(2)}, u32[]{:S(2)}) collective-permute-start(bf16[128,576]{0,1:T(8,128)(2,1)S(1)} %collective-permute-done.5), channel_id=1, source_target_pairs={{0,64},{8,72},{16,80},{24,88},{32,96},{40,104},{48,112},{56,120},{... | collective-permute-start | bytes 442376 | tf_op jit(solution)/shard_map/ppermute | solution.py:17
  208.7 3.5 copy-start.29
  226.2 8.2 copy-start.56
  226.2 56.8 %copy-start.20 = (bf16[128,1536]{1,0:T(8,128)(2,1)S(1)}, bf16[128,1536]{1,0:T(8,128)(2,1)}, u32[]{:S(2)}) copy-start(bf16[128,1536]{1,0:T(8,128)(2,1)} %param.12) | copy-start | bytes 1179652
  226.2 605.6 %copy-start.1 = (bf16[512,2048]{1,0:T(8,128)(2,1)S(1)}, bf16[512,2048]{1,0:T(8,128)(2,1)}, u32[]{:S(2)}) copy-start(bf16[512,2048]{1,0:T(8,128)(2,1)} %param.15) | copy-start | bytes 6291460
  (39 other events, 62.1 us)
Sparse Core Ops, SparseCore 0:
  31.0 127.7 all-gather.1
  285.0 540.5 all-reduce.4
